TPU v7x, 256 devices: a whole 4x4x8 slice. The times are simulated.
256 devices in a mesh: probe: 64 (over z, x_lo, y), slab: 4 (over x_hi, core).
Axes of the slice: x: 4 (x_hi: 2, x_lo: 2; x = x_hi * 2 + x_lo), y: 4, z: 8, core: 2. Of those that a mesh axis runs over, the one named last changes fastest.
Arguments:
- smatrix: bfloat16 [2, 512, 128, 128], P(None, 'probe', 'slab'), may hold values from -6 to 6
- amplitude: float32 [2, 512], replicated, may hold values from -0.25 to 0.25
- beam_index: int32 [512, 2], replicated, may hold values from -32 to 31
- positions: int32 [8192, 2], P('probe'), may hold values from -8 to 8
Outputs:
- patterns: float32 [8192, 128, 128], P('probe', 'slab')
Inputs may be any that keep to these rules, and one draw needn't show every extreme that they name: `positions`: column 0 is the row offset that places a probe's crop in the band, column 1 the column offset. `beam_index`: column 0 along rows, column 1 along columns.
All inputs are finite; a program needn't handle non-finite values.
Results may differ from a plain program's by a relative error of at most 0.0029.
Values may be sent and summed in bfloat16 or wider, within the bound.
A program may use at most 128 MiB of HBM per device.

v0:
```python
import math
import jax
import jax.numpy as jnp
from jax import lax
from jax.sharding import PartitionSpec as P

HALO = 8


def padded_2(x, sides, width):
    for axis, dim in sides:
        count, length = (lax.axis_size(axis), x.shape[dim])
        up = [(i, (i + 1) % count) for i in range(count - 1)]
        down = [(j, i) for i, j in up]
        last = lax.slice_in_dim(x, length - width, length, axis=dim)
        leading = lax.slice_in_dim(x, 0, width, axis=dim)
        before = lax.ppermute(last, axis, up)
        after = lax.ppermute(leading, axis, down)
        x = jnp.concatenate([before, x, after], axis=dim)
    return x


def beam_weights(amplitude, beam_index, place, rows_all, cols):
    row_phase = (
        jnp.mod(place[:, 0:1] * beam_index[None, :, 0], rows_all).astype(jnp.float32) / rows_all
    )
    col_phase = jnp.mod(place[:, 1:2] * beam_index[None, :, 1], cols).astype(jnp.float32) / cols
    angle = 2.0 * math.pi * (row_phase + col_phase)
    cosine = jnp.cos(angle)
    sine = jnp.sin(angle)
    real = amplitude[0][None, :] * cosine + amplitude[1][None, :] * sine
    imag = amplitude[1][None, :] * cosine - amplitude[0][None, :] * sine
    return (real.astype(jnp.bfloat16), imag.astype(jnp.bfloat16))


def dft_table(first, second, length):
    angle = (
        2.0
        * math.pi
        * (jnp.mod(first[:, None] * second[None, :], length).astype(jnp.float32) / length)
    )
    return (jnp.cos(angle), jnp.sin(angle))


def cut_rows(field, offset, count):
    return lax.dynamic_slice_in_dim(field, offset, count, 0)


def on_device(smatrix, amplitude, beam_index, positions):
    slab_rows = smatrix.shape[2]
    cols = smatrix.shape[3]
    rows_all = slab_rows * lax.axis_size("slab")
    probes_here = positions.shape[0]
    tall = slab_rows + 2 * HALO
    band = tall * cols
    highest = lax.Precision.HIGHEST
    weight_re, weight_im = beam_weights(amplitude, beam_index, positions, rows_all, cols)
    padded = padded_2(smatrix, (("slab", 2),), HALO)
    piece = lax.all_gather(padded, "probe", axis=1, tiled=True)
    count = piece.shape[1]
    flat = piece.reshape(2, count, band)
    real = jnp.dot(weight_re, flat[0], preferred_element_type=jnp.float32) - jnp.dot(
        weight_im, flat[1], preferred_element_type=jnp.float32
    )
    imag = jnp.dot(weight_re, flat[1], preferred_element_type=jnp.float32) + jnp.dot(
        weight_im, flat[0], preferred_element_type=jnp.float32
    )
    starts = positions[:, 0] + HALO
    wave_re = jax.vmap(lambda field, offset: cut_rows(field, offset, slab_rows))(
        real.reshape(probes_here, tall, cols), starts
    )
    wave_im = jax.vmap(lambda field, offset: cut_rows(field, offset, slab_rows))(
        imag.reshape(probes_here, tall, cols), starts
    )
    col_index = jnp.arange(cols, dtype=jnp.int32)
    col_cos, col_sin = dft_table(col_index, col_index, cols)
    half_re = jnp.dot(wave_re, col_cos, precision=highest) + jnp.dot(
        wave_im, col_sin, precision=highest
    )
    half_im = jnp.dot(wave_im, col_cos, precision=highest) - jnp.dot(
        wave_re, col_sin, precision=highest
    )
    scale = 1.0 / math.sqrt(rows_all * cols)
    local_rows = lax.axis_index("slab") * slab_rows + jnp.arange(slab_rows, dtype=jnp.int32)
    freq = jnp.arange(lax.axis_size("slab") * slab_rows, dtype=jnp.int32)
    row_cos, row_sin = dft_table(freq, local_rows, rows_all)
    out_re = jnp.einsum("kr,prc->kpc", row_cos, half_re, precision=highest) + jnp.einsum(
        "kr,prc->kpc", row_sin, half_im, precision=highest
    )
    out_im = jnp.einsum("kr,prc->kpc", row_cos, half_im, precision=highest) - jnp.einsum(
        "kr,prc->kpc", row_sin, half_re, precision=highest
    )
    summed = lax.psum_scatter(
        jnp.stack([out_re, out_im], 1) * scale, "slab", scatter_dimension=0, tiled=True
    )
    power = summed[:, 0] ** 2 + summed[:, 1] ** 2
    return jnp.transpose(power, (1, 0, 2))


def solution(mesh):
    return jax.shard_map(
        on_device,
        mesh=mesh,
        in_specs=(P(None, "probe", "slab", None), P(), P(), P("probe", None)),
        out_specs=P("probe", "slab", None),
        check_vma=False,
    )
```

profile of v0, /device:TPU:1, one launch (start us, length us, event | category | flops | bytes accessed | tf_op | source)
XLA Modules:
  0.0 566.4 jit_solution(1741276528891264881)
XLA Ops:
  6.5 0.0 all-gather.2.cloned.1.call-start
  6.5 0.8 fusion.116
  7.3 6.0 %collective-permute-start = (bf16[2,8,8,128]{3,2,1,0:T(8,128)(2,1)S(1)}, bf16[2,8,8,128]{3,2,1,0:T(8,128)(2,1)S(1)}, u32[]{:S(2)}, u32[]{:S(2)}) collective-permute-start(bf16[2,8,8,128]{3,2,1,0:T(8,128)(2,1)S(1)} %get-tuple-element.7), channel_id=1, source_target_pairs={{0,1},{1,2},{2,3},{4,5},{5,6},{6,7},{8,9},{9,10},{10,11},{12,13},{... | collective-permute-start | bytes 98312 | tf_op jit(solution)/shard_map/ppermute | solution.py:17
  13.3 1.9 collective-permute-start.1
  15.3 0.0 collective-permute-done
  15.3 4.8 collective-permute-done.1
  20.1 1.6 pad_maximum_fusion
  21.7 0.0 all-gather.2.cloned.1.call-update
  21.7 0.0 reduce-scatter.2.cloned.1.call-start
  21.8 0.8 or_bitcast_fusion
  22.5 0.8 fusion.117
  23.3 0.8 fusion.118
  24.1 276.4 %all-gather.2.cloned.1.call-done = bf16[2,512,48,128]{3,2,1,0:T(8,128)(2,1)} async-done(((bf16[2,8,48,128]{3,2,1,0:T(8,128)(2,1)}), bf16[2,512,48,128]{3,2,1,0:T(8,128)(2,1)}) %all-gather.2.cloned.1.call-update) | async-done | bytes 12582928 | tf_op jit(solution)/shard_map/all_gather | solution.py:59
  300.5 6.2 %fusion.115 = (bf16[1,512,48,128]{3,2,1,0:T(8,128)(2,1)S(1)}, bf16[1,512,48,128]{3,2,1,0:T(8,128)(2,1)S(1)}) fusion(bf16[2,512,48,128]{3,2,1,0:T(8,128)(2,1)} %all-gather.2.cloned.1.call-done), kind=kLoop, calls=%fused_computation.140 | loop fusion | bytes 25165824 | tf_op jit(solution)/shard_map/slice | solution.py:62
  306.7 2.4 fusion
  309.1 2.4 fusion.4
  311.4 2.6 fusion.21
  314.0 2.6 fusion.18
  316.6 2.0 copy.46
  318.7 0.4 copy.45
  319.1 6.3 %gather_fusion = f32[128,32,128]{2,0,1:T(8,128)} fusion(f32[128,48,128]{2,0,1:T(8,128)} %bitcast.71, s32[128]{0:T(128)S(1)} %get-tuple-element.13), kind=kCustom, calls=%fused_computation | custom fusion | bytes 4195840 | tf_op jit(solution)/shard_map/vmap()/gather | solution.py:46
  325.4 6.2 %gather_fusion.1 = f32[128,32,128]{2,0,1:T(8,128)} fusion(f32[128,48,128]{2,0,1:T(8,128)S(1)} %bitcast.70, s32[128]{0:T(128)S(1)} %get-tuple-element.13), kind=kCustom, calls=%fused_computation.1 | custom fusion | bytes 4195840 | tf_op jit(solution)/shard_map/vmap()/gather | solution.py:46
  331.6 0.0 copy-start.1
  331.6 3.9 fusion.37
  335.5 0.0 copy-done.1
  335.5 2.1 fusion.39
  337.7 0.0 copy-start
  337.7 2.1 convolution_subtract_fusion.1
  339.8 0.0 copy-done
  339.8 2.3 convolution_add_fusion.1
  342.1 7.4 %fusion.16 = f32[128,128,128]{2,0,1:T(8,128)S(1)} fusion(f32[128,32,128]{2,0,1:T(8,128)S(1)} %convolution_add_fusion.1, s32[32]{0:T(128)S(1)} %iota_add_fusion), kind=kOutput, calls=%fused_computation.27 | convolution fusion | flops 805363712 | bytes 10485888 | tf_op jit(solution)/shard_map/kr,prc->kpc/dot_general | solution.py:87
  349.5 7.7 %fusion.12 = f32[128,128,128]{2,0,1:T(8,128)S(1)} fusion(f32[128,32,128]{2,0,1:T(8,128)S(1)} %convolution_subtract_fusion.1, s32[32]{0:T(128)S(1)} %iota_add_fusion), kind=kOutput, calls=%fused_computation.23 | convolution fusion | flops 805363712 | bytes 10485888 | tf_op jit(solution)/shard_map/kr,prc->kpc/dot_general | solution.py:90
  357.2 7.4 %add_bitcast_fusion = f32[128,1,128,128]{3,0,2,1:T(8,128)S(1)} fusion(f32[128,128,128]{2,0,1:T(8,128)S(1)} %fusion.16, f32[128,32,128]{2,0,1:T(8,128)S(1)} %convolution_subtract_fusion.1, s32[32]{0:T(128)S(1)} %iota_add_fusion), kind=kOutput, calls=%fused_computation.4 | convolution fusion | flops 807460864 | bytes 18874496 | tf_op jit(solution)/shard_map/kr,prc->kpc/dot_general | solution.py:87
  364.6 7.7 %subtract_bitcast_fusion = f32[128,1,128,128]{3,0,2,1:T(8,128)S(1)} fusion(f32[128,128,128]{2,0,1:T(8,128)S(1)} %fusion.12, f32[128,32,128]{2,0,1:T(8,128)S(1)} %convolution_add_fusion.1, s32[32]{0:T(128)S(1)} %iota_add_fusion), kind=kOutput, calls=%fused_computation.3 | convolution fusion | flops 807460864 | bytes 18874496 | tf_op jit(solution)/shard_map/kr,prc->kpc/dot_general | solution.py:90
  372.3 6.0 %maximum_multiply_fusion = f32[128,2,128,128]{3,0,2,1:T(8,128)} fusion(f32[128,1,128,128]{3,0,2,1:T(8,128)S(1)} %subtract_bitcast_fusion, f32[128,1,128,128]{3,0,2,1:T(8,128)S(1)} %add_bitcast_fusion), kind=kLoop, calls=%fused_computation.2 | loop fusion | flops 8388608 | bytes 33554432 | tf_op jit(solution)/shard_map/mul | solution.py:94
  378.4 0.0 reduce-scatter.2.cloned.1.call-update
  378.4 176.7 %reduce-scatter.2.cloned.1.call-done = f32[32,2,128,128]{3,0,2,1:T(8,128)} async-done(((f32[128,2,128,128]{3,0,2,1:T(8,128)}), f32[32,2,128,128]{3,0,2,1:T(8,128)}) %reduce-scatter.2.cloned.1.call-update) | async-done | bytes 4194320 | tf_op jit(solution)/shard_map/reduce_scatter | solution.py:93
  555.1 4.0 fusion.11
  (1 shorter events, 0.0 us)
Async XLA Ops:
  6.5 294.0 %all-gather.2.cloned.1.call-start = ((), (), s32[]{:S(2)}) async-start(), calls=%async_computation.1 | async-start | bytes 12779520 | tf_op jit(solution)/shard_map/all_gather | solution.py:59
  7.3 8.0 %collective-permute-start = (bf16[2,8,8,128]{3,2,1,0:T(8,128)(2,1)S(1)}, bf16[2,8,8,128]{3,2,1,0:T(8,128)(2,1)S(1)}, u32[]{:S(2)}, u32[]{:S(2)}) collective-permute-start(bf16[2,8,8,128]{3,2,1,0:T(8,128)(2,1)S(1)} %get-tuple-element.7), channel_id=1, source_target_pairs={{0,1},{1,2},{2,3},{4,5},{5,6},{6,7},{8,9},{9,10},{10,11},{12,13},{... | collective-permute-start | bytes 98312 | tf_op jit(solution)/shard_map/ppermute | solution.py:17
  13.3 6.7 %collective-permute-start.1 = (bf16[2,8,8,128]{3,2,1,0:T(8,128)(2,1)S(1)}, bf16[2,8,8,128]{3,2,1,0:T(8,128)(2,1)S(1)}, u32[]{:S(2)}, u32[]{:S(2)}) collective-permute-start(bf16[2,8,8,128]{3,2,1,0:T(8,128)(2,1)S(1)} %get-tuple-element.8), channel_id=1, source_target_pairs={{1,0},{2,1},{3,2},{5,4},{6,5},{7,6},{9,8},{10,9},{11,10},{13,12},{... | collective-permute-start | bytes 98312 | tf_op jit(solution)/shard_map/ppermute | solution.py:18
  21.7 533.4 %reduce-scatter.2.cloned.1.call-start = ((), (), s32[]{:S(2)}) async-start(), calls=%async_computation.2 | async-start | bytes 20971520 | tf_op jit(solution)/shard_map/reduce_scatter | solution.py:93
  331.6 3.9 copy-start.1
  337.7 2.1 copy-start
Sparse Core Ops, SparseCore 0:
  21.8 278.6 all-gather.1
  378.5 176.5 reduce-scatter.1
where the time goes:
time: 576 us; the launch traced here: 566 us
  waiting for transfers between devices  458 us (80%)
  matrix products  50.5 us (9%)
  local copies, waits for them, and re-layouts  23.5 us (4%)
  between operations  14 us (2%)
  other arithmetic  12.5 us (2%)
  starting transfers between devices  7.98 us (1%)
    all_gather x1, waiting for transfers between devices, on_device(): piece = lax.all_gather(padded, 'probe', axis=1, tiled=True)  276 us
    reduce_scatter x1, waiting for transfers between devices, on_device(): lax.psum_scatter(jnp.stack([out_re, out_im], 1) * scale, 'slab', scatter_...  177 us
    gather x2, local copies, waits for them, and re-layouts, cut_rows(): return lax.dynamic_slice_in_dim(field, offset, count, 0)  12.6 us
  transfers between devices with their start and end apart: 4, of which 3 were waited for; matrix products, arithmetic and copies ran while one was open for 0% of the time, Pallas kernels for 0%

commit v1 on v0

--- a/solution.py
+++ b/solution.py
@@ -5,6 +5,13 @@
 from jax.sharding import PartitionSpec as P
 
 HALO = 8
+
+
+def settle_sizes(block_in, named_axis):
+    buffer = []
+    for _ in range(lax.axis_size(named_axis)):
+        buffer.append(block_in)
+    return jnp.concatenate(lax.all_to_all(jnp.stack(buffer), named_axis, 0, 0), axis=1)
 
 
 def padded_2(x, sides, width):
@@ -56,7 +63,7 @@
     highest = lax.Precision.HIGHEST
     weight_re, weight_im = beam_weights(amplitude, beam_index, positions, rows_all, cols)
     padded = padded_2(smatrix, (("slab", 2),), HALO)
-    piece = lax.all_gather(padded, "probe", axis=1, tiled=True)
+    piece = settle_sizes(padded, "probe")
     count = piece.shape[1]
     flat = piece.reshape(2, count, band)
     real = jnp.dot(weight_re, flat[0], preferred_element_type=jnp.float32) - jnp.dot(

time: 576 us -> 539 us (0.936)
  waiting for transfers between devices: 458 us -> 409 us
  starting transfers between devices: 7.98 us -> 20.2 us
  local copies, waits for them, and re-layouts: 23.5 us -> 30 us
    all_gather x1 -> x0, waiting for transfers between devices: 276 us -> none  [on_device(): piece = lax.all_gather(padded, 'probe', axis=1, tiled=True)]
    all_to_all x0 -> x1, waiting for transfers between devices: none -> 272 us  [settle_sizes(): lax.all_to_all(jnp.stack(buffer), named_axis, 0, 0)]
    reduce_scatter x1, waiting for transfers between devices: 177 us -> 133 us  [on_device(): lax.psum_scatter(jnp.stack([out_re, out_im], 1) * scale, 'slab', scatter_...]
    all_to_all x0 -> x1, starting transfers between devices: none -> 12.2 us  [settle_sizes(): lax.all_to_all(jnp.stack(buffer), named_axis, 0, 0)]
    another operation x0 -> x1, local copies, waits for them, and re-layouts: none -> 7.61 us  [settle_sizes(): jnp.stack(buffer)]
    unnamed x4 -> x11, local copies, waits for them, and re-layouts: 0.01 us -> 6.73 us
    slice x1 -> x0, local copies, waits for them, and re-layouts: 6.15 us -> none  [on_device(): flat[0]]
where the time goes in v1:
time: 539 us; the launch traced here: 535 us
  waiting for transfers between devices  409 us (76%)
  matrix products  50.7 us (9%)
  local copies, waits for them, and re-layouts  30 us (6%)
  starting transfers between devices  20.2 us (4%)
  between operations  13.9 us (3%)
  other arithmetic  11 us (2%)
    all_to_all x1, waiting for transfers between devices, settle_sizes(): lax.all_to_all(jnp.stack(buffer), named_axis, 0, 0)  272 us
    reduce_scatter x1, waiting for transfers between devices, on_device(): lax.psum_scatter(jnp.stack([out_re, out_im], 1) * scale, 'slab', scatter_...  133 us
    gather x2, local copies, waits for them, and re-layouts, cut_rows(): return lax.dynamic_slice_in_dim(field, offset, count, 0)  12.4 us
    all_to_all x1, starting transfers between devices, settle_sizes(): lax.all_to_all(jnp.stack(buffer), named_axis, 0, 0)  12.2 us
  transfers between devices with their start and end apart: 4, of which 3 were waited for; matrix products, arithmetic and copies ran while one was open for 0% of the time, Pallas kernels for 0%

profile of v1, /device:TPU:1, one launch (start us, length us, event | category | flops | bytes accessed | tf_op | source)
XLA Modules:
  0.0 535.0 jit_solution(4978994689818359028)
XLA Ops:
  6.5 0.8 fusion.115
  7.3 6.0 %collective-permute-start = (bf16[2,8,8,128]{3,2,1,0:T(8,128)(2,1)S(1)}, bf16[2,8,8,128]{3,2,1,0:T(8,128)(2,1)S(1)}, u32[]{:S(2)}, u32[]{:S(2)}) collective-permute-start(bf16[2,8,8,128]{3,2,1,0:T(8,128)(2,1)S(1)} %get-tuple-element.7), channel_id=1, source_target_pairs={{0,1},{1,2},{2,3},{4,5},{5,6},{6,7},{8,9},{9,10},{10,11},{12,13},{... | collective-permute-start | bytes 98312 | tf_op jit(solution)/shard_map/ppermute | solution.py:24
  13.3 1.9 collective-permute-start.1
  15.3 0.0 collective-permute-done
  15.3 4.8 collective-permute-done.1
  20.1 0.9 pad_maximum_fusion
  21.0 7.6 %stack.8 = bf16[64,2,8,48,128]{4,3,2,1,0:T(8,128)(2,1)} broadcast(bf16[2,8,48,128]{3,2,1,0:T(8,128)(2,1)S(1)} %pad_maximum_fusion), dimensions={1,2,3,4} | broadcast | bytes 12779520 | tf_op jit(solution)/shard_map/stack | solution.py:14
  28.6 0.0 copy-start.4
  28.6 0.0 copy-start.2
  28.6 0.0 copy-start.3
  28.6 12.2 %all-to-all-start = ((bf16[64,2,8,48,128]{4,3,2,1,0:T(8,128)(2,1)}), bf16[64,2,8,48,128]{4,3,2,1,0:T(8,128)(2,1)}, u32[]{:S(2)}, u32[]{:S(2)}) async-start(bf16[64,2,8,48,128]{4,3,2,1,0:T(8,128)(2,1)} %stack.8), calls=%async_computation | async-start | bytes 25165824 | tf_op jit(solution)/shard_map/all_to_all | solution.py:14
  40.9 0.0 reduce-scatter.2.cloned.1.call-start
  40.9 0.0 copy-done.4
  40.9 0.0 copy-done.2
  41.0 0.0 copy-done.3
  41.0 271.9 %all-to-all-done = bf16[64,2,8,48,128]{4,3,2,1,0:T(8,128)(2,1)} async-done(((bf16[64,2,8,48,128]{4,3,2,1,0:T(8,128)(2,1)}), bf16[64,2,8,48,128]{4,3,2,1,0:T(8,128)(2,1)}, u32[]{:S(2)}, u32[]{:S(2)}) %all-to-all-start) | async-done | bytes 12582944 | tf_op jit(solution)/shard_map/all_to_all | solution.py:14
  312.9 6.7 %slice_bitcast_fusion.1 = (bf16[64,8,48,128]{3,2,1,0:T(8,128)(2,1)S(1)}, bf16[64,8,48,128]{3,2,1,0:T(8,128)(2,1)S(1)}) fusion(bf16[2,64,8,48,128]{4,3,2,0,1:T(8,128)(2,1)} %bitcast.7), kind=kLoop, calls=%fused_computation.14 | loop fusion | bytes 25165824
  319.6 2.4 fusion.4
  322.0 2.4 fusion
  324.4 2.6 fusion.18
  327.0 2.6 fusion.21
  329.6 2.0 copy.45
  331.6 0.4 copy.46
  332.0 6.2 %gather_fusion.1 = f32[128,32,128]{2,0,1:T(8,128)} fusion(f32[128,48,128]{2,0,1:T(8,128)} %bitcast.76, s32[128]{0:T(128)S(1)} %get-tuple-element.13), kind=kCustom, calls=%fused_computation.1 | custom fusion | bytes 4195840 | tf_op jit(solution)/shard_map/vmap()/gather | solution.py:53
  338.2 6.3 %gather_fusion = f32[128,32,128]{2,0,1:T(8,128)} fusion(f32[128,48,128]{2,0,1:T(8,128)S(1)} %bitcast.75, s32[128]{0:T(128)S(1)} %get-tuple-element.13), kind=kCustom, calls=%fused_computation | custom fusion | bytes 4195840 | tf_op jit(solution)/shard_map/vmap()/gather | solution.py:53
  344.5 0.0 copy-start.1
  344.5 3.8 fusion.39
  348.3 0.0 copy-done.1
  348.3 2.1 fusion.37
  350.5 0.0 copy-start
  350.5 2.1 convolution_add_fusion.1
  352.6 0.0 copy-done
  352.6 2.5 convolution_subtract_fusion.1
  355.2 7.4 %fusion.12 = f32[128,128,128]{2,0,1:T(8,128)S(1)} fusion(f32[128,32,128]{2,0,1:T(8,128)S(1)} %convolution_subtract_fusion.1, s32[32]{0:T(128)S(1)} %iota_add_fusion), kind=kOutput, calls=%fused_computation.25 | convolution fusion | flops 805363712 | bytes 10485888 | tf_op jit(solution)/shard_map/kr,prc->kpc/dot_general | solution.py:97
  362.6 7.6 %fusion.16 = f32[128,128,128]{2,0,1:T(8,128)S(1)} fusion(f32[128,32,128]{2,0,1:T(8,128)S(1)} %convolution_add_fusion.1, s32[32]{0:T(128)S(1)} %iota_add_fusion), kind=kOutput, calls=%fused_computation.29 | convolution fusion | flops 805363712 | bytes 10485888 | tf_op jit(solution)/shard_map/kr,prc->kpc/dot_general | solution.py:94
  370.2 7.4 %subtract_bitcast_fusion = f32[128,1,128,128]{3,0,2,1:T(8,128)S(1)} fusion(f32[128,128,128]{2,0,1:T(8,128)S(1)} %fusion.12, f32[128,32,128]{2,0,1:T(8,128)S(1)} %convolution_add_fusion.1, s32[32]{0:T(128)S(1)} %iota_add_fusion), kind=kOutput, calls=%fused_computation.3 | convolution fusion | flops 807460864 | bytes 18874496 | tf_op jit(solution)/shard_map/kr,prc->kpc/dot_general | solution.py:97
  377.6 7.7 %add_bitcast_fusion = f32[128,1,128,128]{3,0,2,1:T(8,128)S(1)} fusion(f32[128,128,128]{2,0,1:T(8,128)S(1)} %fusion.16, f32[128,32,128]{2,0,1:T(8,128)S(1)} %convolution_subtract_fusion.1, s32[32]{0:T(128)S(1)} %iota_add_fusion), kind=kOutput, calls=%fused_computation.4 | convolution fusion | flops 807460864 | bytes 18874496 | tf_op jit(solution)/shard_map/kr,prc->kpc/dot_general | solution.py:94
  385.3 6.0 %maximum_multiply_fusion = f32[128,2,128,128]{3,0,2,1:T(8,128)} fusion(f32[128,1,128,128]{3,0,2,1:T(8,128)S(1)} %subtract_bitcast_fusion, f32[128,1,128,128]{3,0,2,1:T(8,128)S(1)} %add_bitcast_fusion), kind=kLoop, calls=%fused_computation.2 | loop fusion | flops 8388608 | bytes 33554432 | tf_op jit(solution)/shard_map/mul | solution.py:101
  391.4 0.0 reduce-scatter.2.cloned.1.call-update
  391.4 132.6 %reduce-scatter.2.cloned.1.call-done = f32[32,2,128,128]{3,0,2,1:T(8,128)} async-done(((f32[128,2,128,128]{3,0,2,1:T(8,128)}), f32[32,2,128,128]{3,0,2,1:T(8,128)}) %reduce-scatter.2.cloned.1.call-update) | async-done | bytes 4194320 | tf_op jit(solution)/shard_map/reduce_scatter | solution.py:100
  523.9 4.0 fusion.11
  (4 shorter events, 0.0 us)
Async XLA Ops:
  7.3 8.0 %collective-permute-start = (bf16[2,8,8,128]{3,2,1,0:T(8,128)(2,1)S(1)}, bf16[2,8,8,128]{3,2,1,0:T(8,128)(2,1)S(1)}, u32[]{:S(2)}, u32[]{:S(2)}) collective-permute-start(bf16[2,8,8,128]{3,2,1,0:T(8,128)(2,1)S(1)} %get-tuple-element.7), channel_id=1, source_target_pairs={{0,1},{1,2},{2,3},{4,5},{5,6},{6,7},{8,9},{9,10},{10,11},{12,13},{... | collective-permute-start | bytes 98312 | tf_op jit(solution)/shard_map/ppermute | solution.py:24
  13.3 6.7 %collective-permute-start.1 = (bf16[2,8,8,128]{3,2,1,0:T(8,128)(2,1)S(1)}, bf16[2,8,8,128]{3,2,1,0:T(8,128)(2,1)S(1)}, u32[]{:S(2)}, u32[]{:S(2)}) collective-permute-start(bf16[2,8,8,128]{3,2,1,0:T(8,128)(2,1)S(1)} %get-tuple-element.8), channel_id=1, source_target_pairs={{1,0},{2,1},{3,2},{5,4},{6,5},{7,6},{9,8},{10,9},{11,10},{13,12},{... | collective-permute-start | bytes 98312 | tf_op jit(solution)/shard_map/ppermute | solution.py:25
  28.6 12.3 %copy-start.4 = (s32[128,2]{0,1:T(2,128)S(1)}, s32[128,2]{0,1:T(2,128)}, u32[]{:S(2)}) copy-start(s32[128,2]{0,1:T(2,128)} %param.7) | copy-start | bytes 3076
  28.6 12.3 %copy-start.2 = (f32[2,512]{1,0:T(2,128)S(1)}, f32[2,512]{1,0:T(2,128)}, u32[]{:S(2)}) copy-start(f32[2,512]{1,0:T(2,128)} %param.5) | copy-start | bytes 12292
  28.6 12.3 %copy-start.3 = (s32[512,2]{0,1:T(2,128)S(1)}, s32[512,2]{0,1:T(2,128)}, u32[]{:S(2)}) copy-start(s32[512,2]{0,1:T(2,128)} %param.6) | copy-start | bytes 12292
  28.6 284.3 %all-to-all-start = ((bf16[64,2,8,48,128]{4,3,2,1,0:T(8,128)(2,1)}), bf16[64,2,8,48,128]{4,3,2,1,0:T(8,128)(2,1)}, u32[]{:S(2)}, u32[]{:S(2)}) async-start(bf16[64,2,8,48,128]{4,3,2,1,0:T(8,128)(2,1)} %stack.8), calls=%async_computation | async-start | bytes 25165824 | tf_op jit(solution)/shard_map/all_to_all | solution.py:14
  40.9 483.1 %reduce-scatter.2.cloned.1.call-start = ((), (), s32[]{:S(2)}) async-start(), calls=%async_computation.2 | async-start | bytes 20971520 | tf_op jit(solution)/shard_map/reduce_scatter | solution.py:100
  344.5 3.9 copy-start.1
  350.5 2.1 copy-start
Sparse Core Ops, SparseCore 0:
  391.5 132.3 reduce-scatter.1
